TPU v7x, 256 devices: a whole 4x4x8 slice. The times are simulated.
256 devices in a mesh: gx: 4 (over x), gy: 8 (over y, core), gz: 8 (over z).
Axes of the slice: x: 4, y: 4, z: 8, core: 2. Of those that a mesh axis runs over, the one named last changes fastest.
Arguments:
- right_side: float32 [64, 256, 1024], P('gx', 'gy', 'gz'), may hold values from -8 to 8
- diagonal: float32 [64, 256, 1024], P('gx', 'gy', 'gz'), may hold values from 0.16 to 6.1
Outputs:
- solution_field: float32 [64, 256, 1024], P('gx', 'gy', 'gz')
- residual: float32 [64, 256, 1024], P('gx', 'gy', 'gz')
All inputs are finite; a program needn't handle non-finite values.
Results may differ from a plain program's by a relative error of at most 0.0003.
Values sent between devices are 32-bit elements; how exact they have to be, the bound alone decides.
No kernel may reach another device: no remote copies, remote signals or barrier semaphores. Data moves between devices by JAX's collectives and lax.ppermute only.
A program may use at most 128 MiB of HBM per device.

v0:
```python
import jax
import jax.numpy as jnp
from jax import lax
from jax.sharding import Mesh
from jax.sharding import PartitionSpec as P

ITERS = 2
GX_GY_GZ = ("gx", "gy_0", "gy_1", "gz")
GY = ("gy_0", "gy_1")


def extended(cells, sides, width):
    for axis, dim in sides:
        count = lax.axis_size(axis)
        ends = count - 1
        head = lax.slice_in_dim(cells, 0, width, axis=dim)
        tail = lax.slice_in_dim(cells, cells.shape[dim] - width, cells.shape[dim], axis=dim)
        cells = jnp.concatenate(
            [
                lax.ppermute(tail, axis, [(i, (i + 1) % count) for i in range(ends)]),
                cells,
                lax.ppermute(head, axis, [((i + 1) % count, i) for i in range(ends)]),
            ],
            axis=dim,
        )
    return cells


def in_order(tiles, dim):
    tiles = jnp.moveaxis(tiles, 0, dim)
    shape = tiles.shape
    return tiles.reshape(*shape[:dim], shape[dim] * shape[dim + 1], *shape[dim + 2 :])


def one_gather(arrays, axis, dims):
    line = jnp.concatenate([a.reshape(-1) for a in arrays])
    lines, at, outs = (lax.all_gather(line, axis), 0, [])
    for a, dim in zip(arrays, dims):
        tiles = lines[:, at : at + a.size].reshape(-1, *a.shape)
        outs.append(in_order(tiles, dim))
        at += a.size
    return tuple(outs)


def over_axes(array, axes):
    for axis in axes:
        array = lax.psum(array, axis)
    return array


def box_sum(padded):
    total = padded[:-2] + padded[1:-1] + padded[2:]
    total = total[:, :-2] + total[:, 1:-1] + total[:, 2:]
    return total[:, :, :-2] + total[:, :, 1:-1] + total[:, :, 2:]


def operate(field, extra):
    padded = extended(field, (("gx", 0), (GY, 1), ("gz", 2)), 1)
    return (27.0 + extra) * field - box_sum(padded)


def operate_column(field, extra):
    padded = extended(field, (("gx", 0), (GY, 1)), 1)
    padded = jnp.pad(padded, ((0, 0), (0, 0), (1, 1)))
    return (27.0 + extra) * field - box_sum(padded)


def cheb_terms(lower):
    upper = 58.0
    theta = (upper + lower) / 2.0
    delta = (upper - lower) / 2.0
    return (theta, delta, theta / delta)


def smooth(rhs, extra, degree, lower, apply):
    theta, delta, sigma = cheb_terms(lower)
    rho = 1.0 / sigma
    step = rhs / theta
    total = step
    remain = rhs
    for count in range(degree - 1):
        remain = remain - apply(step, extra)
        rho_next = 1.0 / (2.0 * sigma - rho)
        step = rho_next * rho * step + 2.0 * rho_next / delta * remain
        total = total + step
        rho = rho_next
    return total


def blocks(field):
    a, b, c = field.shape
    return field.reshape(a // 2, 2, b // 2, 2, c // 2, 2)


def restrict(field):
    return 0.5 * blocks(field).sum(axis=(1, 3, 5))


def prolong(field):
    a, b, c = field.shape
    wide = jnp.broadcast_to(field[:, None, :, None, :, None], (a, 2, b, 2, c, 2))
    return wide.reshape(2 * a, 2 * b, 2 * c)


def inside_mask(shape):
    places = (lax.axis_index("gx"), lax.axis_index(GY), lax.axis_index("gz"))
    counts = (lax.axis_size("gx"), lax.axis_size(GY), lax.axis_size("gz"))
    result = jnp.ones((1, 1, 1), jnp.float32)
    for dim in range(3):
        count = shape[dim]
        spots = places[dim] * count + jnp.arange(count + 2, dtype=jnp.int32) - 1
        valid = ((spots >= 0) & (spots < counts[dim] * count)).astype(jnp.float32)
        dims_shape = [1, 1, 1]
        dims_shape[dim] = count + 2
        result = result * valid.reshape(dims_shape)
    return result


def deep_pre(r_zero, extra_zero, extra_wide, inside):
    theta, delta, sigma = cheb_terms(7.0)
    rho = 1.0 / sigma
    wide = extended(r_zero, (("gx", 0), (GY, 1), ("gz", 2)), 2)
    step = wide / theta
    middle = step[1:-1, 1:-1, 1:-1]
    extra_mid = extra_wide[1:-1, 1:-1, 1:-1]
    remain = (wide[1:-1, 1:-1, 1:-1] - ((27.0 + extra_mid) * middle - box_sum(step))) * inside
    rho_next = 1.0 / (2.0 * sigma - rho)
    smoothed = middle + (rho_next * rho * middle + 2.0 * rho_next / delta * remain)
    inner = smoothed[1:-1, 1:-1, 1:-1]
    rest = r_zero - ((27.0 + extra_zero) * inner - box_sum(smoothed))
    return (inner, rest)


def coarse_solve(r_two, extra_two):
    whole_r, whole_e = one_gather((r_two, extra_two), "gz", (2, 2))
    solved = smooth(whole_r, whole_e, 3, 1.0, operate_column)
    left = whole_r - operate_column(solved, whole_e)
    shift_line = jnp.sum(left, axis=2, keepdims=True) / jnp.sum(
        1.0 + whole_e, axis=2, keepdims=True
    )
    start = lax.axis_index("gz") * r_two.shape[2]
    return lax.dynamic_slice_in_dim(solved, start, r_two.shape[2], 2) + shift_line


def vcycle(r_zero, extra_zero, extra_one, extra_two, extra_wide, inside):
    z_zero, rest = deep_pre(r_zero, extra_zero, extra_wide, inside)
    r_one = restrict(rest)
    z_one = smooth(r_one, extra_one, 2, 7.0, operate)
    r_two = restrict(r_one - operate(z_one, extra_one))
    z_two = coarse_solve(r_two, extra_two)
    z_one = z_one + prolong(z_two)
    z_one = z_one + smooth(r_one - operate(z_one, extra_one), extra_one, 2, 7.0, operate)
    z_zero = z_zero + prolong(z_one)
    z_zero = z_zero + smooth(r_zero - operate(z_zero, extra_zero), extra_zero, 2, 7.0, operate)
    return z_zero


def local(right_side, diagonal):
    extra_one = blocks(diagonal).mean(axis=(1, 3, 5))
    extra_two = blocks(extra_one).mean(axis=(1, 3, 5))
    extra_wide = None
    inside = None
    extra_wide = extended(diagonal, (("gx", 0), (GY, 1), ("gz", 2)), 2)
    inside = inside_mask(diagonal.shape)
    solution_field = jnp.zeros_like(right_side)
    residual = right_side
    direction = jnp.zeros_like(right_side)
    image = jnp.zeros_like(right_side)
    rz_prev = jnp.float32(1.0)
    curve_prev = jnp.float32(0.0)
    for step in range(ITERS):
        precond = vcycle(residual, diagonal, extra_one, extra_two, extra_wide, inside)
        applied = operate(precond, diagonal)
        rz_now, zw_sum, zq_sum = (
            over_axes(jnp.sum(residual * precond), GX_GY_GZ),
            over_axes(jnp.sum(precond * applied), GX_GY_GZ),
            over_axes(jnp.sum(precond * image), GX_GY_GZ),
        )
        beta = 0.0 if step == 0 else rz_now / rz_prev
        direction = precond + beta * direction
        image = applied + beta * image
        curve = zw_sum + 2.0 * beta * zq_sum + beta * beta * curve_prev
        alpha = rz_now / curve
        solution_field = solution_field + alpha * direction
        residual = residual - alpha * image
        rz_prev = rz_now
        curve_prev = curve
    return (solution_field, residual)


def solution(mesh):
    torus = Mesh(
        mesh.devices.reshape(mesh.shape["gx"], 4, 2, mesh.shape["gz"]), ("gx", "gy_0", "gy_1", "gz")
    )
    in_specs = (P("gx", GY, "gz"), P("gx", GY, "gz"))
    out_specs = (P("gx", GY, "gz"), P("gx", GY, "gz"))
    return jax.shard_map(local, mesh=torus, in_specs=in_specs, out_specs=out_specs, check_vma=False)
```

profile of v0, /device:TPU:2, one launch (start us, length us, event | category | flops | bytes accessed | tf_op | source)
XLA Modules:
  0.0 846.8 jit_solution(9266118594562411616)
XLA Ops:
  1.5 4.2 collective-permute-start.1
  31.9 4.6 collective-permute-start.10
  38.6 4.6 collective-permute-done.5
  47.4 4.6 collective-permute-done.11
  53.9 18.1 %reshape.156 = f32[8,2,16,2,64,2]{5,4,3,2,1,0:T(8,128)} reshape(f32[16,32,128]{2,1,0:T(8,128)S(1)} %fusion.32) | data formatting | bytes 524288 | tf_op jit(solution)/shard_map/reshape | solution.py:92
  72.0 7.0 reduce_sum.158
  91.0 5.8 collective-permute-done.15
  102.1 18.1 %reshape.157 = f32[8,2,16,2,64,2]{5,4,3,2,1,0:T(8,128)} reshape(f32[16,32,128]{2,1,0:T(8,128)S(1)} %copy-done) | data formatting | bytes 524288 | tf_op jit(solution)/shard_map/reshape | solution.py:92
  120.2 7.0 reduce_sum.159
  143.5 5.7 collective-permute-start.22
  151.6 5.3 collective-permute-done.23
  168.4 25.5 %all-gather = f32[16384]{0:T(1024)S(1)} all-gather(f32[2048]{0:T(1024)S(1)} %pad_maximum_fusion.41), channel_id=2, replica_groups=mesh['gx'=4,'gy_0'=4,'gy_1'=2,'gz'=8] {'gz'}, dimensions={0}, use_global_device_ids=true | all-gather | bytes 73728 | tf_op jit(solution)/shard_map/all_gather | solution.py:37
  204.6 5.0 collective-permute-done.27
  226.6 3.9 collective-permute-start.33
  244.9 3.9 collective-permute-start.37
  257.5 4.3 collective-permute-start.40
  264.2 4.5 collective-permute-done.41
  271.0 3.9 collective-permute-start.43
  280.0 4.1 collective-permute-done.45
  290.0 4.5 collective-permute-done.47
  294.8 6.6 broadcast_in_dim.11
  301.4 12.6 %reshape.162 = f32[16,32,128]{2,1,0:T(8,128)S(1)} reshape(f32[8,2,16,2,64,2]{5,4,3,2,1,0:T(8,128)} %broadcast_in_dim.11) | data formatting | bytes 524288 | tf_op jit(solution)/shard_map/reshape | solution.py:102
  316.2 3.9 collective-permute-start.49
  333.8 6.1 collective-permute-done.52
  339.9 4.7 collective-permute-done.53
  347.4 3.9 collective-permute-start.55
  365.0 6.1 collective-permute-done.58
  371.1 4.7 collective-permute-done.59
  378.6 3.9 collective-permute-start.61
  396.3 6.1 collective-permute-done.64
  402.4 4.7 collective-permute-done.65
  408.6 10.4 %all-reduce.11 = (f32[]{:T(128)}, f32[]{:T(128)}, f32[]{:T(128)}) all-reduce(f32[]{:T(128)} %get-tuple-element.7, f32[]{:T(128)} %get-tuple-element.6, f32[]{:T(128)} %get-tuple-element.5), channel_id=1, replica_groups=mesh['gx'=4,'gy_0'=4,'gy_1'=2,'gz'=8] {'gx'}, use_global_device_ids=true, to_apply=%region_8.9 | all-reduce | flops 3 | bytes 24 | tf_op jit(solution)/shard_map/psum | solution.py:47
  419.0 8.9 %all-reduce.9 = (f32[]{:T(128)}, f32[]{:T(128)}, f32[]{:T(128)}) all-reduce(f32[]{:T(128)} %get-tuple-element.23, f32[]{:T(128)} %get-tuple-element.24, f32[]{:T(128)} %get-tuple-element.25), channel_id=1, replica_groups=mesh['gx'=4,'gy_0'=4,'gy_1'=2,'gz'=8] {'gy_0'}, use_global_device_ids=true, to_apply=%region_9.10 | all-reduce | flops 3 | bytes 24 | tf_op jit(solution)/shard_map/psum | solution.py:47
  431.1 16.3 %all-reduce.7 = (f32[]{:T(128)}, f32[]{:T(128)}, f32[]{:T(128)}) all-reduce(f32[]{:T(128)} %get-tuple-element.29, f32[]{:T(128)} %get-tuple-element.30, f32[]{:T(128)} %get-tuple-element.31), channel_id=1, replica_groups=mesh['gx'=4,'gy_0'=4,'gy_1'=2,'gz'=8] {'gz'}, use_global_device_ids=true, to_apply=%region_11.12 | all-reduce | flops 3 | bytes 24 | tf_op jit(solution)/shard_map/psum | solution.py:47
  451.4 3.9 collective-permute-start.67
  467.4 6.9 collective-permute-done.70
  474.3 4.7 collective-permute-done.71
  482.7 18.1 %reshape.163 = f32[8,2,16,2,64,2]{5,4,3,2,1,0:T(8,128)} reshape(f32[16,32,128]{2,1,0:T(8,128)S(1)} %fusion.21) | data formatting | bytes 524288 | tf_op jit(solution)/shard_map/reshape | solution.py:92
  500.8 7.0 reduce_sum.169
  528.9 5.0 collective-permute-done.77
  536.2 3.9 collective-permute-start.79
  545.1 4.2 collective-permute-done.81
  549.5 5.5 collective-permute-start.82
  557.4 4.5 collective-permute-done.83
  567.6 24.8 %all-gather.1 = f32[16384]{0:T(1024)S(1)} all-gather(f32[2048]{0:T(1024)S(1)} %pad_maximum_fusion.40), channel_id=3, replica_groups=mesh['gx'=4,'gy_0'=4,'gy_1'=2,'gz'=8] {'gz'}, dimensions={0}, use_global_device_ids=true | all-gather | bytes 73728 | tf_op jit(solution)/shard_map/all_gather | solution.py:37
  594.7 3.9 collective-permute-start.85
  609.2 3.9 collective-permute-start.89
  661.7 4.5 collective-permute-done.101
  686.5 4.4 collective-permute-done.107
  691.1 6.6 broadcast_in_dim.14
  697.7 12.6 %reshape.168 = f32[16,32,128]{2,1,0:T(8,128)S(1)} reshape(f32[8,2,16,2,64,2]{5,4,3,2,1,0:T(8,128)} %broadcast_in_dim.14) | data formatting | bytes 524288 | tf_op jit(solution)/shard_map/reshape | solution.py:102
  712.5 3.9 collective-permute-start.109
  725.2 4.0 collective-permute-start.112
  730.5 6.1 collective-permute-done.112
  736.6 4.5 collective-permute-done.113
  743.9 3.9 collective-permute-start.115
  761.8 6.1 collective-permute-done.118
  767.9 4.7 collective-permute-done.119
  775.4 3.9 collective-permute-start.121
  791.6 6.1 collective-permute-done.124
  797.7 4.7 collective-permute-done.125
  803.8 10.4 %all-reduce.10 = (f32[]{:T(128)}, f32[]{:T(128)}, f32[]{:T(128)}) all-reduce(f32[]{:T(128)} %get-tuple-element.4, f32[]{:T(128)} %get-tuple-element.3, f32[]{:T(128)} %get-tuple-element.2), channel_id=1, replica_groups=mesh['gx'=4,'gy_0'=4,'gy_1'=2,'gz'=8] {'gx'}, use_global_device_ids=true, to_apply=%region_28.29 | all-reduce | flops 3 | bytes 24 | tf_op jit(solution)/shard_map/psum | solution.py:47
  814.3 8.8 %all-reduce.8 = (f32[]{:T(128)}, f32[]{:T(128)}, f32[]{:T(128)}) all-reduce(f32[]{:T(128)} %get-tuple-element.20, f32[]{:T(128)} %get-tuple-element.21, f32[]{:T(128)} %get-tuple-element.22), channel_id=1, replica_groups=mesh['gx'=4,'gy_0'=4,'gy_1'=2,'gz'=8] {'gy_0'}, use_global_device_ids=true, to_apply=%region_29.30 | all-reduce | flops 3 | bytes 24 | tf_op jit(solution)/shard_map/psum | solution.py:47
  826.3 16.3 %all-reduce.6 = (f32[]{:T(128)}, f32[]{:T(128)}, f32[]{:T(128)}) all-reduce(f32[]{:T(128)} %get-tuple-element.26, f32[]{:T(128)} %get-tuple-element.27, f32[]{:T(128)} %get-tuple-element.28), channel_id=1, replica_groups=mesh['gx'=4,'gy_0'=4,'gy_1'=2,'gz'=8] {'gz'}, use_global_device_ids=true, to_apply=%region_31.32 | all-reduce | flops 3 | bytes 24 | tf_op jit(solution)/shard_map/psum | solution.py:47
  (476 shorter events, 385.9 us)
Async XLA Ops:
  1.5 13.9 %collective-permute-start.1 = (f32[2,32,128]{2,1,0:T(8,128)S(1)}, f32[2,32,128]{2,1,0:T(8,128)S(1)}, u32[]{:S(2)}, u32[]{:S(2)}) collective-permute-start(f32[2,32,128]{2,1,0:T(8,128)S(1)} %get-tuple-element.98), channel_id=1, source_target_pairs={{64,0},{128,64},{192,128},{65,1},{129,65},{193,129},{66,2},{130,66... | collective-permute-start | bytes 98312 | tf_op jit(solution)/shard_map/ppermute | solution.py:22
  5.7 8.7 %collective-permute-start = (f32[2,32,128]{2,1,0:T(8,128)S(1)}, f32[2,32,128]{2,1,0:T(8,128)S(1)}, u32[]{:S(2)}, u32[]{:S(2)}) collective-permute-start(f32[2,32,128]{2,1,0:T(8,128)S(1)} %get-tuple-element.99), channel_id=1, source_target_pairs={{0,64},{64,128},{128,192},{1,65},{65,129},{129,193},{2,66},{66,130... | collective-permute-start | bytes 98312 | tf_op jit(solution)/shard_map/ppermute | solution.py:20
  8.4 13.3 %collective-permute-start.7 = (f32[2,32,128]{2,1,0:T(8,128)S(1)}, f32[2,32,128]{2,1,0:T(8,128)S(1)}, u32[]{:S(2)}, u32[]{:S(2)}) collective-permute-start(f32[2,32,128]{2,1,0:T(8,128)S(1)} %get-tuple-element.96), channel_id=1, source_target_pairs={{64,0},{128,64},{192,128},{65,1},{129,65},{193,129},{66,2},{130,66... | collective-permute-start | bytes 98312 | tf_op jit(solution)/shard_map/ppermute | solution.py:22
  12.3 5.8 collective-permute-start.6
  19.1 7.1 collective-permute-start.2
  20.4 5.8 collective-permute-start.3
  21.7 9.8 %collective-permute-start.8 = (f32[20,2,128]{2,1,0:T(2,128)S(1)}, f32[20,2,128]{2,1,0:T(2,128)S(1)}, u32[]{:S(2)}, u32[]{:S(2)}) collective-permute-start(f32[20,2,128]{2,1,0:T(2,128)S(1)} %get-tuple-element.66), channel_id=1, source_target_pairs={{0,8},{8,16},{16,24},{24,32},{32,40},{40,48},{48,56},{1,9},{9,17},... | collective-permute-start | bytes 61448 | tf_op jit(solution)/shard_map/ppermute | solution.py:20
  24.8 6.7 collective-permute-start.9
  26.4 12.2 %collective-permute-start.4 = (f32[20,36,2]{2,1,0:T(8,128)S(1)}, f32[20,36,2]{2,1,0:T(8,128)S(1)}, u32[]{:S(2)}, u32[]{:S(2)}) collective-permute-start(f32[20,36,2]{2,1,0:T(8,128)S(1)} %get-tuple-element.50), channel_id=1, source_target_pairs={{0,1},{1,2},{2,3},{3,4},{4,5},{5,6},{6,7},{8,9},{9,10},{10,11},{11... | collective-permute-start | bytes 17288 | tf_op jit(solution)/shard_map/ppermute | solution.py:20
  30.3 12.9 %collective-permute-start.5 = (f32[20,36,2]{2,1,0:T(8,128)S(1)}, f32[20,36,2]{2,1,0:T(8,128)S(1)}, u32[]{:S(2)}, u32[]{:S(2)}) collective-permute-start(f32[20,36,2]{2,1,0:T(8,128)S(1)} %get-tuple-element.51), channel_id=1, source_target_pairs={{1,0},{2,1},{3,2},{4,3},{5,4},{6,5},{7,6},{9,8},{10,9},{11,10},{12... | collective-permute-start | bytes 17288 | tf_op jit(solution)/shard_map/ppermute | solution.py:22
  31.9 15.6 %collective-permute-start.10 = (f32[20,36,2]{2,1,0:T(8,128)S(1)}, f32[20,36,2]{2,1,0:T(8,128)S(1)}, u32[]{:S(2)}, u32[]{:S(2)}) collective-permute-start(f32[20,36,2]{2,1,0:T(8,128)S(1)} %get-tuple-element.48), channel_id=1, source_target_pairs={{0,1},{1,2},{2,3},{3,4},{4,5},{5,6},{6,7},{8,9},{9,10},{10,11},{11... | collective-permute-start | bytes 17288 | tf_op jit(solution)/shard_map/ppermute | solution.py:20
  36.4 15.5 %collective-permute-start.11 = (f32[20,36,2]{2,1,0:T(8,128)S(1)}, f32[20,36,2]{2,1,0:T(8,128)S(1)}, u32[]{:S(2)}, u32[]{:S(2)}) collective-permute-start(f32[20,36,2]{2,1,0:T(8,128)S(1)} %get-tuple-element.49), channel_id=1, source_target_pairs={{1,0},{2,1},{3,2},{4,3},{5,4},{6,5},{7,6},{9,8},{10,9},{11,10},{12... | collective-permute-start | bytes 17288 | tf_op jit(solution)/shard_map/ppermute | solution.py:22
  79.1 5.9 collective-permute-start.12
  89.7 7.1 collective-permute-start.15
  97.0 30.3 %collective-permute-start.16 = (f32[10,18,1]{2,1,0:T(8,128)S(1)}, f32[10,18,1]{2,1,0:T(8,128)S(1)}, u32[]{:S(2)}, u32[]{:S(2)}) collective-permute-start(f32[10,18,1]{2,1,0:T(8,128)S(1)} %get-tuple-element.114), channel_id=1, source_target_pairs={{0,1},{1,2},{2,3},{3,4},{4,5},{5,6},{6,7},{8,9},{9,10},{10,11},{11... | collective-permute-start | bytes 2168 | tf_op jit(solution)/shard_map/ppermute | solution.py:20
  100.8 26.4 %collective-permute-start.17 = (f32[10,18,1]{2,1,0:T(8,128)S(1)}, f32[10,18,1]{2,1,0:T(8,128)S(1)}, u32[]{:S(2)}, u32[]{:S(2)}) collective-permute-start(f32[10,18,1]{2,1,0:T(8,128)S(1)} %get-tuple-element.115), channel_id=1, source_target_pairs={{1,0},{2,1},{3,2},{4,3},{5,4},{6,5},{7,6},{9,8},{10,9},{11,10},{12... | collective-permute-start | bytes 2168 | tf_op jit(solution)/shard_map/ppermute | solution.py:22
  127.6 5.9 collective-permute-start.18
  143.5 8.1 collective-permute-start.22
  149.2 7.7 collective-permute-start.23
  194.2 5.9 collective-permute-start.24
  203.0 6.6 collective-permute-start.27
  209.9 5.9 collective-permute-start.28
  224.6 5.9 collective-permute-start.32
  243.0 5.9 collective-permute-start.36
  257.5 6.8 collective-permute-start.40
  261.8 6.9 collective-permute-start.41
  269.1 5.9 collective-permute-start.42
  284.2 5.8 collective-permute-start.46
  287.6 6.9 collective-permute-start.47
  314.2 5.9 collective-permute-start.48
  316.2 5.8 collective-permute-start.49
  328.8 11.1 %collective-permute-start.52 = (f32[18,34,1]{2,1,0:T(8,128)S(1)}, f32[18,34,1]{2,1,0:T(8,128)S(1)}, u32[]{:S(2)}, u32[]{:S(2)}) collective-permute-start(f32[18,34,1]{2,1,0:T(8,128)S(1)} %get-tuple-element.62), channel_id=1, source_target_pairs={{0,1},{1,2},{2,3},{3,4},{4,5},{5,6},{6,7},{8,9},{9,10},{10,11},{11... | collective-permute-start | bytes 7352 | tf_op jit(solution)/shard_map/ppermute | solution.py:20
  332.5 12.2 %collective-permute-start.53 = (f32[18,34,1]{2,1,0:T(8,128)S(1)}, f32[18,34,1]{2,1,0:T(8,128)S(1)}, u32[]{:S(2)}, u32[]{:S(2)}) collective-permute-start(f32[18,34,1]{2,1,0:T(8,128)S(1)} %get-tuple-element.63), channel_id=1, source_target_pairs={{1,0},{2,1},{3,2},{4,3},{5,4},{6,5},{7,6},{9,8},{10,9},{11,10},{12... | collective-permute-start | bytes 7352 | tf_op jit(solution)/shard_map/ppermute | solution.py:22
  345.5 5.9 collective-permute-start.54
  360.3 10.9 %collective-permute-start.58 = (f32[18,34,1]{2,1,0:T(8,128)S(1)}, f32[18,34,1]{2,1,0:T(8,128)S(1)}, u32[]{:S(2)}, u32[]{:S(2)}) collective-permute-start(f32[18,34,1]{2,1,0:T(8,128)S(1)} %get-tuple-element.60), channel_id=1, source_target_pairs={{0,1},{1,2},{2,3},{3,4},{4,5},{5,6},{6,7},{8,9},{9,10},{10,11},{11... | collective-permute-start | bytes 7352 | tf_op jit(solution)/shard_map/ppermute | solution.py:20
  363.7 12.2 %collective-permute-start.59 = (f32[18,34,1]{2,1,0:T(8,128)S(1)}, f32[18,34,1]{2,1,0:T(8,128)S(1)}, u32[]{:S(2)}, u32[]{:S(2)}) collective-permute-start(f32[18,34,1]{2,1,0:T(8,128)S(1)} %get-tuple-element.61), channel_id=1, source_target_pairs={{1,0},{2,1},{3,2},{4,3},{5,4},{6,5},{7,6},{9,8},{10,9},{11,10},{12... | collective-permute-start | bytes 7352 | tf_op jit(solution)/shard_map/ppermute | solution.py:22
  376.7 5.9 collective-permute-start.60
  391.3 11.1 %collective-permute-start.64 = (f32[18,34,1]{2,1,0:T(8,128)S(1)}, f32[18,34,1]{2,1,0:T(8,128)S(1)}, u32[]{:S(2)}, u32[]{:S(2)}) collective-permute-start(f32[18,34,1]{2,1,0:T(8,128)S(1)} %get-tuple-element.58), channel_id=1, source_target_pairs={{0,1},{1,2},{2,3},{3,4},{4,5},{5,6},{6,7},{8,9},{9,10},{10,11},{11... | collective-permute-start | bytes 7352 | tf_op jit(solution)/shard_map/ppermute | solution.py:20
  395.0 12.2 %collective-permute-start.65 = (f32[18,34,1]{2,1,0:T(8,128)S(1)}, f32[18,34,1]{2,1,0:T(8,128)S(1)}, u32[]{:S(2)}, u32[]{:S(2)}) collective-permute-start(f32[18,34,1]{2,1,0:T(8,128)S(1)} %get-tuple-element.59), channel_id=1, source_target_pairs={{1,0},{2,1},{3,2},{4,3},{5,4},{6,5},{7,6},{9,8},{10,9},{11,10},{12... | collective-permute-start | bytes 7352 | tf_op jit(solution)/shard_map/ppermute | solution.py:22
  449.4 5.9 collective-permute-start.66
  451.4 5.8 collective-permute-start.67
  463.6 10.7 %collective-permute-start.70 = (f32[20,36,2]{2,1,0:T(8,128)S(1)}, f32[20,36,2]{2,1,0:T(8,128)S(1)}, u32[]{:S(2)}, u32[]{:S(2)}) collective-permute-start(f32[20,36,2]{2,1,0:T(8,128)S(1)} %get-tuple-element.46), channel_id=1, source_target_pairs={{0,1},{1,2},{2,3},{3,4},{4,5},{5,6},{6,7},{8,9},{9,10},{10,11},{11... | collective-permute-start | bytes 17288 | tf_op jit(solution)/shard_map/ppermute | solution.py:20
  466.1 12.9 %collective-permute-start.71 = (f32[20,36,2]{2,1,0:T(8,128)S(1)}, f32[20,36,2]{2,1,0:T(8,128)S(1)}, u32[]{:S(2)}, u32[]{:S(2)}) collective-permute-start(f32[20,36,2]{2,1,0:T(8,128)S(1)} %get-tuple-element.47), channel_id=1, source_target_pairs={{1,0},{2,1},{3,2},{4,3},{5,4},{6,5},{7,6},{9,8},{10,9},{11,10},{12... | collective-permute-start | bytes 17288 | tf_op jit(solution)/shard_map/ppermute | solution.py:22
  507.9 5.9 collective-permute-start.72
  526.5 7.5 collective-permute-start.77
  534.3 5.9 collective-permute-start.78
  549.5 7.9 collective-permute-start.82
  555.0 6.9 collective-permute-start.83
  592.7 5.9 collective-permute-start.84
  607.2 5.9 collective-permute-start.88
  621.9 5.9 collective-permute-start.92
  641.7 5.9 collective-permute-start.96
  659.3 6.9 collective-permute-start.101
  666.6 5.9 collective-permute-start.102
  684.1 6.8 collective-permute-start.107
  710.5 5.9 collective-permute-start.108
  725.2 11.4 %collective-permute-start.112 = (f32[18,34,1]{2,1,0:T(8,128)S(1)}, f32[18,34,1]{2,1,0:T(8,128)S(1)}, u32[]{:S(2)}, u32[]{:S(2)}) collective-permute-start(f32[18,34,1]{2,1,0:T(8,128)S(1)} %get-tuple-element.56), channel_id=1, source_target_pairs={{0,1},{1,2},{2,3},{3,4},{4,5},{5,6},{6,7},{8,9},{9,10},{10,11},{11... | collective-permute-start | bytes 7352 | tf_op jit(solution)/shard_map/ppermute | solution.py:20
  729.2 11.9 %collective-permute-start.113 = (f32[18,34,1]{2,1,0:T(8,128)S(1)}, f32[18,34,1]{2,1,0:T(8,128)S(1)}, u32[]{:S(2)}, u32[]{:S(2)}) collective-permute-start(f32[18,34,1]{2,1,0:T(8,128)S(1)} %get-tuple-element.57), channel_id=1, source_target_pairs={{1,0},{2,1},{3,2},{4,3},{5,4},{6,5},{7,6},{9,8},{10,9},{11,10},{12... | collective-permute-start | bytes 7352 | tf_op jit(solution)/shard_map/ppermute | solution.py:22
  742.0 5.9 collective-permute-start.114
  756.8 11.1 %collective-permute-start.118 = (f32[18,34,1]{2,1,0:T(8,128)S(1)}, f32[18,34,1]{2,1,0:T(8,128)S(1)}, u32[]{:S(2)}, u32[]{:S(2)}) collective-permute-start(f32[18,34,1]{2,1,0:T(8,128)S(1)} %get-tuple-element.54), channel_id=1, source_target_pairs={{0,1},{1,2},{2,3},{3,4},{4,5},{5,6},{6,7},{8,9},{9,10},{10,11},{11... | collective-permute-start | bytes 7352 | tf_op jit(solution)/shard_map/ppermute | solution.py:20
  760.5 12.2 %collective-permute-start.119 = (f32[18,34,1]{2,1,0:T(8,128)S(1)}, f32[18,34,1]{2,1,0:T(8,128)S(1)}, u32[]{:S(2)}, u32[]{:S(2)}) collective-permute-start(f32[18,34,1]{2,1,0:T(8,128)S(1)} %get-tuple-element.55), channel_id=1, source_target_pairs={{1,0},{2,1},{3,2},{4,3},{5,4},{6,5},{7,6},{9,8},{10,9},{11,10},{12... | collective-permute-start | bytes 7352 | tf_op jit(solution)/shard_map/ppermute | solution.py:22
  773.5 5.9 collective-permute-start.120
  787.1 10.6 %collective-permute-start.124 = (f32[18,34,1]{2,1,0:T(8,128)S(1)}, f32[18,34,1]{2,1,0:T(8,128)S(1)}, u32[]{:S(2)}, u32[]{:S(2)}) collective-permute-start(f32[18,34,1]{2,1,0:T(8,128)S(1)} %get-tuple-element.52), channel_id=1, source_target_pairs={{0,1},{1,2},{2,3},{3,4},{4,5},{5,6},{6,7},{8,9},{9,10},{10,11},{11... | collective-permute-start | bytes 7352 | tf_op jit(solution)/shard_map/ppermute | solution.py:20
  790.3 12.2 %collective-permute-start.125 = (f32[18,34,1]{2,1,0:T(8,128)S(1)}, f32[18,34,1]{2,1,0:T(8,128)S(1)}, u32[]{:S(2)}, u32[]{:S(2)}) collective-permute-start(f32[18,34,1]{2,1,0:T(8,128)S(1)} %get-tuple-element.53), channel_id=1, source_target_pairs={{1,0},{2,1},{3,2},{4,3},{5,4},{6,5},{7,6},{9,8},{10,9},{11,10},{12... | collective-permute-start | bytes 7352 | tf_op jit(solution)/shard_map/ppermute | solution.py:22
  (78 other events, 1384.5 us)
where the time goes:
time: 859 us; the launch traced here: 847 us
  starting transfers between devices  302 us (35%)
  waiting for transfers between devices  243 us (28%)
  blocking collectives  128 us (15%)
  local copies, waits for them, and re-layouts  118 us (14%)
  other arithmetic  47 us (5%)
  between operations  8.84 us (1%)
    ppermute x63, waiting for transfers between devices, extended(): lax.ppermute(head, axis, [((i + 1) % count, i) for i in range(ends)])  184 us
    ppermute x63, starting transfers between devices, extended(): lax.ppermute(tail, axis, [(i, (i + 1) % count) for i in range(ends)])  164 us
    ppermute x63, starting transfers between devices, extended(): lax.ppermute(head, axis, [((i + 1) % count, i) for i in range(ends)])  138 us
    psum x8, blocking collectives, over_axes(): array = lax.psum(array, axis)  77.4 us
    reshape x5, local copies, waits for them, and re-layouts, blocks(): return field.reshape(a // 2, 2, b // 2, 2, c // 2, 2)  60.8 us
    ppermute x63, waiting for transfers between devices, extended(): lax.ppermute(tail, axis, [(i, (i + 1) % count) for i in range(ends)])  58.3 us
    all_gather x2, blocking collectives, one_gather(): lines, at, outs = (lax.all_gather(line, axis), 0, [])  50.3 us
    reshape x4, local copies, waits for them, and re-layouts, prolong(): return wide.reshape(2 * a, 2 * b, 2 * c)  30.8 us
  transfers between devices with their start and end apart: 126, of which 75 were waited for; matrix products, arithmetic and copies ran while one was open for 4% of the time, Pallas kernels for 0%

commit v1 on v0

--- a/solution.py
+++ b/solution.py
@@ -44,7 +44,7 @@
 
 def over_axes(array, axes):
     for axis in axes:
-        array = lax.psum(array, axis)
+        array = jnp.sum(lax.all_gather(array, axis), axis=0)
     return array
 
 

time: 859 us -> 902 us (1.050)
  local copies, waits for them, and re-layouts: 118 us -> 154 us
  other arithmetic: 47 us -> 61.8 us
    psum x8 -> x0, blocking collectives: 77.4 us -> none  [over_axes(): array = lax.psum(array, axis)]
    unnamed x0 -> x8, blocking collectives: none -> 71.9 us
    unnamed x36 -> x94, local copies, waits for them, and re-layouts: 2.01 us -> 38 us
    reduce_sum x0 -> x24, other arithmetic: none -> 14.7 us  [over_axes(): array = jnp.sum(lax.all_gather(array, axis), axis=0)]
  transfers between devices with their start and end apart: 126 -> 126, of which waited for: 75 -> 74; matrix products, arithmetic and copies ran while one was open for 4% -> 3% of each run, Pallas kernels for 0% -> 0%
where the time goes in v1:
time: 902 us; the launch traced here: 890 us
  starting transfers between devices  304 us (34%)
  waiting for transfers between devices  239 us (26%)
  local copies, waits for them, and re-layouts  154 us (17%)
  blocking collectives  122 us (14%)
  other arithmetic  61.8 us (7%)
  between operations  9.04 us (1%)
    ppermute x63, waiting for transfers between devices, extended(): lax.ppermute(head, axis, [((i + 1) % count, i) for i in range(ends)])  184 us
    ppermute x63, starting transfers between devices, extended(): lax.ppermute(tail, axis, [(i, (i + 1) % count) for i in range(ends)])  168 us
    ppermute x63, starting transfers between devices, extended(): lax.ppermute(head, axis, [((i + 1) % count, i) for i in range(ends)])  136 us
    unnamed x8, blocking collectives  71.9 us
    reshape x5, local copies, waits for them, and re-layouts, blocks(): return field.reshape(a // 2, 2, b // 2, 2, c // 2, 2)  60.7 us
    ppermute x63, waiting for transfers between devices, extended(): lax.ppermute(tail, axis, [(i, (i + 1) % count) for i in range(ends)])  54.7 us
    all_gather x2, blocking collectives, one_gather(): lines, at, outs = (lax.all_gather(line, axis), 0, [])  50.1 us
    unnamed x94, local copies, waits for them, and re-layouts  38 us
  transfers between devices with their start and end apart: 126, of which 74 were waited for; matrix products, arithmetic and copies ran while one was open for 3% of the time, Pallas kernels for 0%

profile of v1, /device:TPU:2, one launch (start us, length us, event | category | flops | bytes accessed | tf_op | source)
XLA Modules:
  0.0 889.6 jit_solution(1407139920446362880)
XLA Ops:
  18.8 4.8 collective-permute-start.8
  30.7 4.6 collective-permute-start.10
  37.4 4.6 collective-permute-done.5
  46.2 4.6 collective-permute-done.11
  52.7 18.1 %reshape.156 = f32[8,2,16,2,64,2]{5,4,3,2,1,0:T(8,128)} reshape(f32[16,32,128]{2,1,0:T(8,128)S(1)} %fusion.32) | data formatting | bytes 524288 | tf_op jit(solution)/shard_map/reshape | solution.py:92
  70.8 7.0 reduce_sum.374
  89.8 5.8 collective-permute-done.15
  100.9 18.1 %reshape.157 = f32[8,2,16,2,64,2]{5,4,3,2,1,0:T(8,128)} reshape(f32[16,32,128]{2,1,0:T(8,128)S(1)} %copy-done) | data formatting | bytes 524288 | tf_op jit(solution)/shard_map/reshape | solution.py:92
  118.9 7.0 reduce_sum.375
  142.0 5.7 collective-permute-start.22
  150.1 5.3 collective-permute-done.23
  166.8 25.5 %all-gather = f32[16384]{0:T(1024)S(1)} all-gather(f32[2048]{0:T(1024)S(1)} %pad_maximum_fusion.41), channel_id=2, replica_groups=mesh['gx'=4,'gy_0'=4,'gy_1'=2,'gz'=8] {'gz'}, dimensions={0}, use_global_device_ids=true | all-gather | bytes 73728 | tf_op jit(solution)/shard_map/all_gather | solution.py:37
  194.6 3.9 collective-permute-start.25
  203.1 5.0 collective-permute-done.27
  210.3 3.9 collective-permute-start.29
  225.0 3.9 collective-permute-start.33
  243.3 3.9 collective-permute-start.37
  255.9 4.3 collective-permute-start.40
  262.7 4.5 collective-permute-done.41
  278.4 4.1 collective-permute-done.45
  288.5 4.5 collective-permute-done.47
  293.3 6.5 broadcast_in_dim.11
  299.8 12.6 %reshape.162 = f32[16,32,128]{2,1,0:T(8,128)S(1)} reshape(f32[8,2,16,2,64,2]{5,4,3,2,1,0:T(8,128)} %broadcast_in_dim.11) | data formatting | bytes 524288 | tf_op jit(solution)/shard_map/reshape | solution.py:102
  314.6 3.9 collective-permute-start.49
  332.2 6.1 collective-permute-done.52
  338.3 4.7 collective-permute-done.53
  345.8 3.9 collective-permute-start.55
  363.3 6.1 collective-permute-done.58
  369.4 4.7 collective-permute-done.59
  376.9 3.9 collective-permute-start.61
  395.2 5.5 collective-permute-done.64
  400.7 4.7 collective-permute-done.65
  411.7 9.7 %all-reduce.35 = (f32[4]{0:T(128)S(1)}, f32[4]{0:T(128)S(1)}, f32[4]{0:T(128)S(1)}) all-reduce(f32[4]{0:T(128)S(1)} %dynamic-update-slice, f32[4]{0:T(128)S(1)} %dynamic-update-slice.4, f32[4]{0:T(128)S(1)} %dynamic-update-slice.8), channel_id=1, replica_groups=mesh['gx'=4,'gy_0'=4,'gy_1'=2,'gz'=8] {'gx'}, use_global_device_ids=true, to_apply=%add.6 | all-reduce | flops 12 | bytes 96
  428.1 8.2 all-reduce.33
  451.6 15.6 %all-reduce.31 = (f32[8]{0:T(128)S(1)}, f32[8]{0:T(128)S(1)}, f32[8]{0:T(128)S(1)}) all-reduce(f32[8]{0:T(128)S(1)} %dynamic-update-slice.3, f32[8]{0:T(128)S(1)} %dynamic-update-slice.7, f32[8]{0:T(128)S(1)} %dynamic-update-slice.11), channel_id=1, replica_groups=mesh['gx'=4,'gy_0'=4,'gy_1'=2,'gz'=8] {'gz'}, use_global_device_ids=true, to_apply=%add.9 | all-reduce | flops 24 | bytes 192
  473.0 3.9 collective-permute-start.67
  489.0 6.9 collective-permute-done.70
  495.9 4.7 collective-permute-done.71
  504.4 18.1 %reshape.163 = f32[8,2,16,2,64,2]{5,4,3,2,1,0:T(8,128)} reshape(f32[16,32,128]{2,1,0:T(8,128)S(1)} %fusion.21) | data formatting | bytes 524288 | tf_op jit(solution)/shard_map/reshape | solution.py:92
  522.5 7.0 reduce_sum.397
  550.5 5.0 collective-permute-done.77
  557.8 3.9 collective-permute-start.79
  566.7 4.2 collective-permute-done.81
  571.1 5.5 collective-permute-start.82
  579.0 4.5 collective-permute-done.83
  589.2 24.6 %all-gather.1 = f32[16384]{0:T(1024)S(1)} all-gather(f32[2048]{0:T(1024)S(1)} %pad_maximum_fusion.40), channel_id=3, replica_groups=mesh['gx'=4,'gy_0'=4,'gy_1'=2,'gz'=8] {'gz'}, dimensions={0}, use_global_device_ids=true | all-gather | bytes 73728 | tf_op jit(solution)/shard_map/all_gather | solution.py:37
  616.1 3.9 collective-permute-start.85
  683.1 4.5 collective-permute-done.101
  707.9 4.4 collective-permute-done.107
  712.5 6.5 broadcast_in_dim.14
  719.0 12.6 %reshape.168 = f32[16,32,128]{2,1,0:T(8,128)S(1)} reshape(f32[8,2,16,2,64,2]{5,4,3,2,1,0:T(8,128)} %broadcast_in_dim.14) | data formatting | bytes 524288 | tf_op jit(solution)/shard_map/reshape | solution.py:102
  733.8 3.9 collective-permute-start.109
  746.6 4.0 collective-permute-start.112
  751.8 6.1 collective-permute-done.112
  758.0 4.5 collective-permute-done.113
  765.2 3.9 collective-permute-start.115
  783.3 6.0 collective-permute-done.118
  789.2 4.7 collective-permute-done.119
  796.8 3.9 collective-permute-start.121
  812.9 6.1 collective-permute-done.124
  819.0 4.7 collective-permute-done.125
  829.4 9.7 %all-reduce.34 = (f32[4]{0:T(128)S(1)}, f32[4]{0:T(128)S(1)}, f32[4]{0:T(128)S(1)}) all-reduce(f32[4]{0:T(128)S(1)} %dynamic-update-slice.12, f32[4]{0:T(128)S(1)} %dynamic-update-slice.16, f32[4]{0:T(128)S(1)} %dynamic-update-slice.20), channel_id=1, replica_groups=mesh['gx'=4,'gy_0'=4,'gy_1'=2,'gz'=8] {'gx'}, use_global_device_ids=true, to_apply=%add.18 | all-reduce | flops 12 | bytes 96
  845.1 8.2 all-reduce.32
  867.7 15.6 %all-reduce.30 = (f32[8]{0:T(128)S(1)}, f32[8]{0:T(128)S(1)}, f32[8]{0:T(128)S(1)}) all-reduce(f32[8]{0:T(128)S(1)} %dynamic-update-slice.15, f32[8]{0:T(128)S(1)} %dynamic-update-slice.19, f32[8]{0:T(128)S(1)} %dynamic-update-slice.23), channel_id=1, replica_groups=mesh['gx'=4,'gy_0'=4,'gy_1'=2,'gz'=8] {'gz'}, use_global_device_ids=true, to_apply=%add.21 | all-reduce | flops 24 | bytes 192
  (558 shorter events, 433.2 us)
Async XLA Ops:
  1.5 12.6 %collective-permute-start = (f32[2,32,128]{2,1,0:T(8,128)S(1)}, f32[2,32,128]{2,1,0:T(8,128)S(1)}, u32[]{:S(2)}, u32[]{:S(2)}) collective-permute-start(f32[2,32,128]{2,1,0:T(8,128)S(1)} %get-tuple-element.99), channel_id=1, source_target_pairs={{0,64},{64,128},{128,192},{1,65},{65,129},{129,193},{2,66},{66,130... | collective-permute-start | bytes 98312 | tf_op jit(solution)/shard_map/ppermute | solution.py:20
  4.9 10.2 %collective-permute-start.1 = (f32[2,32,128]{2,1,0:T(8,128)S(1)}, f32[2,32,128]{2,1,0:T(8,128)S(1)}, u32[]{:S(2)}, u32[]{:S(2)}) collective-permute-start(f32[2,32,128]{2,1,0:T(8,128)S(1)} %get-tuple-element.98), channel_id=1, source_target_pairs={{64,0},{128,64},{192,128},{65,1},{129,65},{193,129},{66,2},{130,66... | collective-permute-start | bytes 98312 | tf_op jit(solution)/shard_map/ppermute | solution.py:22
  8.1 9.6 %collective-permute-start.6 = (f32[2,32,128]{2,1,0:T(8,128)S(1)}, f32[2,32,128]{2,1,0:T(8,128)S(1)}, u32[]{:S(2)}, u32[]{:S(2)}) collective-permute-start(f32[2,32,128]{2,1,0:T(8,128)S(1)} %get-tuple-element.97), channel_id=1, source_target_pairs={{0,64},{64,128},{128,192},{1,65},{65,129},{129,193},{2,66},{66,130... | collective-permute-start | bytes 98312 | tf_op jit(solution)/shard_map/ppermute | solution.py:20
  11.5 7.2 collective-permute-start.7
  15.1 9.8 %collective-permute-start.2 = (f32[20,2,128]{2,1,0:T(2,128)S(1)}, f32[20,2,128]{2,1,0:T(2,128)S(1)}, u32[]{:S(2)}, u32[]{:S(2)}) collective-permute-start(f32[20,2,128]{2,1,0:T(2,128)S(1)} %get-tuple-element.68), channel_id=1, source_target_pairs={{0,8},{8,16},{16,24},{24,32},{32,40},{40,48},{48,56},{1,9},{9,17},... | collective-permute-start | bytes 61448 | tf_op jit(solution)/shard_map/ppermute | solution.py:20
  16.4 8.5 collective-permute-start.3
  18.8 11.6 %collective-permute-start.8 = (f32[20,2,128]{2,1,0:T(2,128)S(1)}, f32[20,2,128]{2,1,0:T(2,128)S(1)}, u32[]{:S(2)}, u32[]{:S(2)}) collective-permute-start(f32[20,2,128]{2,1,0:T(2,128)S(1)} %get-tuple-element.66), channel_id=1, source_target_pairs={{0,8},{8,16},{16,24},{24,32},{32,40},{40,48},{48,56},{1,9},{9,17},... | collective-permute-start | bytes 61448 | tf_op jit(solution)/shard_map/ppermute | solution.py:20
  23.6 6.7 collective-permute-start.9
  25.2 12.2 %collective-permute-start.4 = (f32[20,36,2]{2,1,0:T(8,128)S(1)}, f32[20,36,2]{2,1,0:T(8,128)S(1)}, u32[]{:S(2)}, u32[]{:S(2)}) collective-permute-start(f32[20,36,2]{2,1,0:T(8,128)S(1)} %get-tuple-element.50), channel_id=1, source_target_pairs={{0,1},{1,2},{2,3},{3,4},{4,5},{5,6},{6,7},{8,9},{9,10},{10,11},{11... | collective-permute-start | bytes 17288 | tf_op jit(solution)/shard_map/ppermute | solution.py:20
  29.1 12.9 %collective-permute-start.5 = (f32[20,36,2]{2,1,0:T(8,128)S(1)}, f32[20,36,2]{2,1,0:T(8,128)S(1)}, u32[]{:S(2)}, u32[]{:S(2)}) collective-permute-start(f32[20,36,2]{2,1,0:T(8,128)S(1)} %get-tuple-element.51), channel_id=1, source_target_pairs={{1,0},{2,1},{3,2},{4,3},{5,4},{6,5},{7,6},{9,8},{10,9},{11,10},{12... | collective-permute-start | bytes 17288 | tf_op jit(solution)/shard_map/ppermute | solution.py:22
  30.7 15.6 %collective-permute-start.10 = (f32[20,36,2]{2,1,0:T(8,128)S(1)}, f32[20,36,2]{2,1,0:T(8,128)S(1)}, u32[]{:S(2)}, u32[]{:S(2)}) collective-permute-start(f32[20,36,2]{2,1,0:T(8,128)S(1)} %get-tuple-element.48), channel_id=1, source_target_pairs={{0,1},{1,2},{2,3},{3,4},{4,5},{5,6},{6,7},{8,9},{9,10},{10,11},{11... | collective-permute-start | bytes 17288 | tf_op jit(solution)/shard_map/ppermute | solution.py:20
  35.2 15.5 %collective-permute-start.11 = (f32[20,36,2]{2,1,0:T(8,128)S(1)}, f32[20,36,2]{2,1,0:T(8,128)S(1)}, u32[]{:S(2)}, u32[]{:S(2)}) collective-permute-start(f32[20,36,2]{2,1,0:T(8,128)S(1)} %get-tuple-element.49), channel_id=1, source_target_pairs={{1,0},{2,1},{3,2},{4,3},{5,4},{6,5},{7,6},{9,8},{10,9},{11,10},{12... | collective-permute-start | bytes 17288 | tf_op jit(solution)/shard_map/ppermute | solution.py:22
  77.9 5.9 collective-permute-start.12
  88.5 7.1 collective-permute-start.15
  95.7 30.2 %collective-permute-start.16 = (f32[10,18,1]{2,1,0:T(8,128)S(1)}, f32[10,18,1]{2,1,0:T(8,128)S(1)}, u32[]{:S(2)}, u32[]{:S(2)}) collective-permute-start(f32[10,18,1]{2,1,0:T(8,128)S(1)} %get-tuple-element.114), channel_id=1, source_target_pairs={{0,1},{1,2},{2,3},{3,4},{4,5},{5,6},{6,7},{8,9},{9,10},{10,11},{11... | collective-permute-start | bytes 2168 | tf_op jit(solution)/shard_map/ppermute | solution.py:20
  99.6 26.4 %collective-permute-start.17 = (f32[10,18,1]{2,1,0:T(8,128)S(1)}, f32[10,18,1]{2,1,0:T(8,128)S(1)}, u32[]{:S(2)}, u32[]{:S(2)}) collective-permute-start(f32[10,18,1]{2,1,0:T(8,128)S(1)} %get-tuple-element.115), channel_id=1, source_target_pairs={{1,0},{2,1},{3,2},{4,3},{5,4},{6,5},{7,6},{9,8},{10,9},{11,10},{12... | collective-permute-start | bytes 2168 | tf_op jit(solution)/shard_map/ppermute | solution.py:22
  126.3 5.9 collective-permute-start.18
  142.0 8.1 collective-permute-start.22
  147.7 7.7 collective-permute-start.23
  192.7 5.9 collective-permute-start.24
  201.5 6.6 collective-permute-start.27
  208.4 5.9 collective-permute-start.28
  223.1 5.9 collective-permute-start.32
  241.4 5.9 collective-permute-start.36
  255.9 6.8 collective-permute-start.40
  260.3 6.9 collective-permute-start.41
  267.5 5.9 collective-permute-start.42
  282.7 5.8 collective-permute-start.46
  286.0 6.9 collective-permute-start.47
  312.7 5.9 collective-permute-start.48
  314.6 5.8 collective-permute-start.49
  327.2 11.1 %collective-permute-start.52 = (f32[18,34,1]{2,1,0:T(8,128)S(1)}, f32[18,34,1]{2,1,0:T(8,128)S(1)}, u32[]{:S(2)}, u32[]{:S(2)}) collective-permute-start(f32[18,34,1]{2,1,0:T(8,128)S(1)} %get-tuple-element.62), channel_id=1, source_target_pairs={{0,1},{1,2},{2,3},{3,4},{4,5},{5,6},{6,7},{8,9},{9,10},{10,11},{11... | collective-permute-start | bytes 7352 | tf_op jit(solution)/shard_map/ppermute | solution.py:20
  330.9 12.2 %collective-permute-start.53 = (f32[18,34,1]{2,1,0:T(8,128)S(1)}, f32[18,34,1]{2,1,0:T(8,128)S(1)}, u32[]{:S(2)}, u32[]{:S(2)}) collective-permute-start(f32[18,34,1]{2,1,0:T(8,128)S(1)} %get-tuple-element.63), channel_id=1, source_target_pairs={{1,0},{2,1},{3,2},{4,3},{5,4},{6,5},{7,6},{9,8},{10,9},{11,10},{12... | collective-permute-start | bytes 7352 | tf_op jit(solution)/shard_map/ppermute | solution.py:22
  343.9 5.9 collective-permute-start.54
  358.6 10.9 %collective-permute-start.58 = (f32[18,34,1]{2,1,0:T(8,128)S(1)}, f32[18,34,1]{2,1,0:T(8,128)S(1)}, u32[]{:S(2)}, u32[]{:S(2)}) collective-permute-start(f32[18,34,1]{2,1,0:T(8,128)S(1)} %get-tuple-element.60), channel_id=1, source_target_pairs={{0,1},{1,2},{2,3},{3,4},{4,5},{5,6},{6,7},{8,9},{9,10},{10,11},{11... | collective-permute-start | bytes 7352 | tf_op jit(solution)/shard_map/ppermute | solution.py:20
  362.0 12.2 %collective-permute-start.59 = (f32[18,34,1]{2,1,0:T(8,128)S(1)}, f32[18,34,1]{2,1,0:T(8,128)S(1)}, u32[]{:S(2)}, u32[]{:S(2)}) collective-permute-start(f32[18,34,1]{2,1,0:T(8,128)S(1)} %get-tuple-element.61), channel_id=1, source_target_pairs={{1,0},{2,1},{3,2},{4,3},{5,4},{6,5},{7,6},{9,8},{10,9},{11,10},{12... | collective-permute-start | bytes 7352 | tf_op jit(solution)/shard_map/ppermute | solution.py:22
  375.0 5.9 collective-permute-start.60
  389.6 11.1 %collective-permute-start.64 = (f32[18,34,1]{2,1,0:T(8,128)S(1)}, f32[18,34,1]{2,1,0:T(8,128)S(1)}, u32[]{:S(2)}, u32[]{:S(2)}) collective-permute-start(f32[18,34,1]{2,1,0:T(8,128)S(1)} %get-tuple-element.58), channel_id=1, source_target_pairs={{0,1},{1,2},{2,3},{3,4},{4,5},{5,6},{6,7},{8,9},{9,10},{10,11},{11... | collective-permute-start | bytes 7352 | tf_op jit(solution)/shard_map/ppermute | solution.py:20
  393.3 12.2 %collective-permute-start.65 = (f32[18,34,1]{2,1,0:T(8,128)S(1)}, f32[18,34,1]{2,1,0:T(8,128)S(1)}, u32[]{:S(2)}, u32[]{:S(2)}) collective-permute-start(f32[18,34,1]{2,1,0:T(8,128)S(1)} %get-tuple-element.59), channel_id=1, source_target_pairs={{1,0},{2,1},{3,2},{4,3},{5,4},{6,5},{7,6},{9,8},{10,9},{11,10},{12... | collective-permute-start | bytes 7352 | tf_op jit(solution)/shard_map/ppermute | solution.py:22
  471.1 5.9 collective-permute-start.66
  473.0 5.8 collective-permute-start.67
  485.2 10.7 %collective-permute-start.70 = (f32[20,36,2]{2,1,0:T(8,128)S(1)}, f32[20,36,2]{2,1,0:T(8,128)S(1)}, u32[]{:S(2)}, u32[]{:S(2)}) collective-permute-start(f32[20,36,2]{2,1,0:T(8,128)S(1)} %get-tuple-element.46), channel_id=1, source_target_pairs={{0,1},{1,2},{2,3},{3,4},{4,5},{5,6},{6,7},{8,9},{9,10},{10,11},{11... | collective-permute-start | bytes 17288 | tf_op jit(solution)/shard_map/ppermute | solution.py:20
  487.7 12.9 %collective-permute-start.71 = (f32[20,36,2]{2,1,0:T(8,128)S(1)}, f32[20,36,2]{2,1,0:T(8,128)S(1)}, u32[]{:S(2)}, u32[]{:S(2)}) collective-permute-start(f32[20,36,2]{2,1,0:T(8,128)S(1)} %get-tuple-element.47), channel_id=1, source_target_pairs={{1,0},{2,1},{3,2},{4,3},{5,4},{6,5},{7,6},{9,8},{10,9},{11,10},{12... | collective-permute-start | bytes 17288 | tf_op jit(solution)/shard_map/ppermute | solution.py:22
  529.5 5.9 collective-permute-start.72
  548.1 7.5 collective-permute-start.77
  555.9 5.9 collective-permute-start.78
  571.1 7.9 collective-permute-start.82
  576.6 6.9 collective-permute-start.83
  614.1 5.9 collective-permute-start.84
  628.6 5.9 collective-permute-start.88
  643.3 5.9 collective-permute-start.92
  663.1 5.9 collective-permute-start.96
  680.7 6.9 collective-permute-start.101
  688.0 5.9 collective-permute-start.102
  705.4 6.8 collective-permute-start.107
  731.9 5.9 collective-permute-start.108
  746.6 11.4 %collective-permute-start.112 = (f32[18,34,1]{2,1,0:T(8,128)S(1)}, f32[18,34,1]{2,1,0:T(8,128)S(1)}, u32[]{:S(2)}, u32[]{:S(2)}) collective-permute-start(f32[18,34,1]{2,1,0:T(8,128)S(1)} %get-tuple-element.56), channel_id=1, source_target_pairs={{0,1},{1,2},{2,3},{3,4},{4,5},{5,6},{6,7},{8,9},{9,10},{10,11},{11... | collective-permute-start | bytes 7352 | tf_op jit(solution)/shard_map/ppermute | solution.py:20
  750.5 11.9 %collective-permute-start.113 = (f32[18,34,1]{2,1,0:T(8,128)S(1)}, f32[18,34,1]{2,1,0:T(8,128)S(1)}, u32[]{:S(2)}, u32[]{:S(2)}) collective-permute-start(f32[18,34,1]{2,1,0:T(8,128)S(1)} %get-tuple-element.57), channel_id=1, source_target_pairs={{1,0},{2,1},{3,2},{4,3},{5,4},{6,5},{7,6},{9,8},{10,9},{11,10},{12... | collective-permute-start | bytes 7352 | tf_op jit(solution)/shard_map/ppermute | solution.py:22
  763.3 5.9 collective-permute-start.114
  778.1 11.1 %collective-permute-start.118 = (f32[18,34,1]{2,1,0:T(8,128)S(1)}, f32[18,34,1]{2,1,0:T(8,128)S(1)}, u32[]{:S(2)}, u32[]{:S(2)}) collective-permute-start(f32[18,34,1]{2,1,0:T(8,128)S(1)} %get-tuple-element.54), channel_id=1, source_target_pairs={{0,1},{1,2},{2,3},{3,4},{4,5},{5,6},{6,7},{8,9},{9,10},{10,11},{11... | collective-permute-start | bytes 7352 | tf_op jit(solution)/shard_map/ppermute | solution.py:20
  781.8 12.2 %collective-permute-start.119 = (f32[18,34,1]{2,1,0:T(8,128)S(1)}, f32[18,34,1]{2,1,0:T(8,128)S(1)}, u32[]{:S(2)}, u32[]{:S(2)}) collective-permute-start(f32[18,34,1]{2,1,0:T(8,128)S(1)} %get-tuple-element.55), channel_id=1, source_target_pairs={{1,0},{2,1},{3,2},{4,3},{5,4},{6,5},{7,6},{9,8},{10,9},{11,10},{12... | collective-permute-start | bytes 7352 | tf_op jit(solution)/shard_map/ppermute | solution.py:22
  794.8 5.9 collective-permute-start.120
  808.4 10.6 %collective-permute-start.124 = (f32[18,34,1]{2,1,0:T(8,128)S(1)}, f32[18,34,1]{2,1,0:T(8,128)S(1)}, u32[]{:S(2)}, u32[]{:S(2)}) collective-permute-start(f32[18,34,1]{2,1,0:T(8,128)S(1)} %get-tuple-element.52), channel_id=1, source_target_pairs={{0,1},{1,2},{2,3},{3,4},{4,5},{5,6},{6,7},{8,9},{9,10},{10,11},{11... | collective-permute-start | bytes 7352 | tf_op jit(solution)/shard_map/ppermute | solution.py:20
  811.6 12.2 %collective-permute-start.125 = (f32[18,34,1]{2,1,0:T(8,128)S(1)}, f32[18,34,1]{2,1,0:T(8,128)S(1)}, u32[]{:S(2)}, u32[]{:S(2)}) collective-permute-start(f32[18,34,1]{2,1,0:T(8,128)S(1)} %get-tuple-element.53), channel_id=1, source_target_pairs={{1,0},{2,1},{3,2},{4,3},{5,4},{6,5},{7,6},{9,8},{10,9},{11,10},{12... | collective-permute-start | bytes 7352 | tf_op jit(solution)/shard_map/ppermute | solution.py:22
  (81 other events, 1899.1 us)
